TPU v7x, 32 devices: a whole 2x2x4 slice. The times are simulated.
32 devices in a mesh: groups: 2 (over x), loop: 16 (over z, y, core).
Axes of the slice: x: 2, y: 2, z: 4, core: 2. Of those that a mesh axis runs over, the one named last changes fastest.
Arguments:
- queries: bfloat16 [256, 4, 64, 128], P(('groups', 'loop')), parts along dimension 0, may hold values from -16 to 16
- new_keys: bfloat16 [256, 4, 4, 128], P(('groups', 'loop')), parts along dimension 0, may hold values from -8 to 8
- new_values: bfloat16 [256, 4, 4, 128], P(('groups', 'loop')), parts along dimension 0, may hold values from -12 to 12
- suffix_keys: bfloat16 [256, 256, 4, 128], P(('groups', 'loop')), parts along dimension 0, may hold values from -8 to 8
- suffix_values: bfloat16 [256, 256, 4, 128], P(('groups', 'loop')), parts along dimension 0, may hold values from -12 to 12
- suffix_len: int32 [256], P(('groups', 'loop')), parts along dimension 0, may hold values from 1 to 256, 16384 in all
- prefix_keys: bfloat16 [32, 64, 4, 128], P(('groups', 'loop')), parts along dimension 0, may hold values from -8 to 8
- prefix_values: bfloat16 [32, 64, 4, 128], P(('groups', 'loop')), parts along dimension 0, may hold values from -12 to 12
- block_ids: int32 [32], P(('groups', 'loop')), parts along dimension 0, may hold values from 0 to 15, each once
- block_lists: int32 [256, 4], P(('groups', 'loop')), parts along dimension 0, may hold values from 0 to 15, all different within a row
Outputs:
- attended: bfloat16 [256, 4, 64, 128], P(('groups', 'loop')), parts along dimension 0
There are 2 independent parts, one for each index of `groups`. A program takes and returns all parts, laid end to end along the dimension named above; each array names one. Nothing has to cross between parts.
Inputs may be any that keep to these rules, and one draw needn't show every extreme that they name: `block_ids`: each slot holds a different block. `block_lists`: each request names 4 different blocks; every block is named by some request. `suffix_len`: some request uses all 256 slots.
All inputs are finite; a program needn't handle non-finite values. No bound on the sum of `suffix_len` on one device may be relied on, other than what follows from the above.
Results may differ from a plain program's by a relative error of at most 0.004.
Values may be sent and summed in bfloat16 or wider, within the bound.
No kernel may reach another device: no remote copies, remote signals or barrier semaphores. Data moves between devices by JAX's collectives and lax.ppermute only.
A program may use at most 64 MiB of HBM per device.

v0:
```python
import math
import jax
import jax.numpy as jnp
from jax import lax
from jax.sharding import PartitionSpec as P


def per_device(
    queries,
    new_keys,
    new_values,
    suffix_keys,
    suffix_values,
    suffix_len,
    prefix_keys,
    prefix_values,
    block_ids,
    block_lists,
):
    requests, decode_steps, head_count, head_width = queries.shape
    key_heads = new_keys.shape[2]
    group_size = head_count // key_heads
    score_scale = 1.0 / math.sqrt(head_width)
    per_request = decode_steps * group_size
    grouped = queries.reshape(requests, decode_steps, key_heads, group_size, head_width)
    grouped = grouped.transpose(0, 2, 1, 3, 4).reshape(requests, key_heads, per_request, head_width)
    suffix_scores = (
        jnp.einsum("rgmd,rkgd->rgmk", grouped, suffix_keys, preferred_element_type=jnp.float32)
        * score_scale
    )
    suffix_slots = suffix_keys.shape[1]
    suffix_shown = (jnp.arange(suffix_slots)[None, :] < suffix_len[:, None])[:, None, None, :]
    fresh_scores = (
        jnp.einsum("rgmd,rtgd->rgmt", grouped, new_keys, preferred_element_type=jnp.float32)
        * score_scale
    )
    step_of_row = jnp.arange(per_request) // group_size
    fresh_shown = (jnp.arange(decode_steps)[None, :] <= step_of_row[:, None])[None, None]
    local_top = jnp.maximum(
        jnp.max(jnp.where(suffix_shown, suffix_scores, -jnp.inf), axis=-1),
        jnp.max(jnp.where(fresh_shown, fresh_scores, -jnp.inf), axis=-1),
    )
    gathered = (
        lax.all_gather(prefix_keys, "loop", axis=0, tiled=True),
        lax.all_gather(prefix_values, "loop", axis=0, tiled=True),
        lax.all_gather(block_ids, "loop", axis=0, tiled=True),
    )
    all_keys, all_values, all_ids = gathered
    block_count = all_ids.shape[0]
    named_count = block_lists.shape[1]
    block_size = all_keys.shape[1]
    matches = all_ids[None, None, :] == block_lists[:, :, None]
    slots = jnp.sum(
        jnp.where(matches, jnp.arange(block_count, dtype=jnp.int32)[None, None, :], 0), axis=2
    )
    prior_keys = all_keys[slots].reshape(requests, named_count * block_size, key_heads, head_width)
    prior_values = all_values[slots].reshape(
        requests, named_count * block_size, key_heads, head_width
    )
    prior_scores = (
        jnp.einsum("rgmd,rkgd->rgmk", grouped, prior_keys, preferred_element_type=jnp.float32)
        * score_scale
    )
    whole_top = jnp.maximum(local_top, jnp.max(prior_scores, axis=-1))
    suffix_weights = jnp.where(suffix_shown, jnp.exp(suffix_scores - whole_top[..., None]), 0.0)
    fresh_weights = jnp.where(fresh_shown, jnp.exp(fresh_scores - whole_top[..., None]), 0.0)
    sums = jnp.sum(suffix_weights, axis=-1) + jnp.sum(fresh_weights, axis=-1)
    weighted = jnp.einsum(
        "rgmk,rkgd->rgmd",
        suffix_weights.astype(jnp.bfloat16),
        suffix_values,
        preferred_element_type=jnp.float32,
    )
    weighted = weighted + jnp.einsum(
        "rgmt,rtgd->rgmd",
        fresh_weights.astype(jnp.bfloat16),
        new_values,
        preferred_element_type=jnp.float32,
    )
    sums, weighted = (sums, weighted)
    prior_weights = jnp.exp(prior_scores - whole_top[..., None])
    sums = sums + jnp.sum(prior_weights, axis=-1)
    weighted = weighted + jnp.einsum(
        "rgmk,rkgd->rgmd",
        prior_weights.astype(jnp.bfloat16),
        prior_values,
        preferred_element_type=jnp.float32,
    )
    mixed = weighted / sums[..., None]
    mixed = mixed.reshape(requests, key_heads, decode_steps, group_size, head_width).transpose(
        0, 2, 1, 3, 4
    )
    return mixed.reshape(requests, decode_steps, head_count, head_width).astype(jnp.bfloat16)


def solution(mesh):
    in_specs = (
        P(("groups", "loop"), None, None, None),
        P(("groups", "loop"), None, None, None),
        P(("groups", "loop"), None, None, None),
        P(("groups", "loop"), None, None, None),
        P(("groups", "loop"), None, None, None),
        P(("groups", "loop")),
        P(("groups", "loop"), None, None, None),
        P(("groups", "loop"), None, None, None),
        P(("groups", "loop")),
        P(("groups", "loop"), None),
    )
    out_specs = P(("groups", "loop"), None, None, None)
    return jax.shard_map(
        per_device, mesh=mesh, in_specs=in_specs, out_specs=out_specs, check_vma=False
    )
```

profile of v0, /device:TPU:0, one launch (start us, length us, event | category | flops | bytes accessed | tf_op | source)
XLA Modules:
  0.0 106.5 jit_solution(6860243202798953930)
XLA Ops:
  6.5 1.6 %copy.70 = bf16[1,64,4,128]{3,1,2,0:T(8,128)(2,1)} copy(bf16[1,64,4,128]{3,2,1,0:T(4,128)(2,1)} %param.16) | data formatting | bytes 131072 | tf_op args[6]
  8.2 0.0 all-gather.3.cloned.1.call-update
  8.2 0.0 all-gather.5.cloned.1.call-start
  8.2 1.5 %copy.76 = bf16[1,64,4,128]{3,1,2,0:T(8,128)(2,1)} copy(bf16[1,64,4,128]{3,2,1,0:T(4,128)(2,1)} %param.17) | data formatting | bytes 131072 | tf_op args[7]
  9.7 0.0 all-gather.5.cloned.1.call-update
  10.4 1.3 %dynamic-slice = u32[1]{0:T(128)} dynamic-slice(u32[32]{0:T(128)} %constant.41, u32[]{:T(128)S(6)} %add.41), dynamic_slice_sizes={1} | dynamic-slice | bytes 12
  11.7 0.7 dynamic-update-slice
  12.4 1.1 %copy.67 = bf16[8,4,4,16,128]{4,3,2,1,0:T(8,128)(2,1)S(1)} copy(bf16[8,4,4,16,128]{4,3,1,2,0:T(8,128)(2,1)} %bitcast.41) | data formatting | bytes 1048576 | tf_op jit(solution)/shard_map/transpose | solution.py:26
  13.5 13.8 %all-reduce = s32[16]{0:T(128)S(1)} all-reduce(s32[16]{0:T(128)S(1)} %dynamic-update-slice), channel_id=1, replica_groups=mesh['groups'=2,'loop'=16] {'loop'}, use_global_device_ids=true, to_apply=%add | all-reduce | flops 16 | bytes 128
  27.3 0.9 select_reduce_fusion.2
  28.2 0.1 copy.71
  28.3 0.1 reshape.102
  28.4 0.7 iota_compare_fusion
  29.1 1.2 %select_reduce_fusion.1 = (f32[8,4,64]{2,1,0:T(4,128)S(1)}, f32[8,4,64,4]{2,3,1,0:T(4,128)S(1)}) fusion(pred[64,4]{0,1:T(4,128)(4,1)S(1)} %iota_compare_fusion.1, bf16[8,4,64,128]{3,2,1,0:T(8,128)(2,1)S(1)} %bitcast.37, bf16[8,4,4,128]{3,2,1,0:T(4,128)(2,1)} %param.11), kind=kOutput, calls=%fused_computation.31 | convolution fusion | flops 2119680 | bytes 598272 | tf_op jit(solution)/shard_map/rgmd,rtgd->rgmt/dot_general | solution.py:34
  30.3 2.2 %select_reduce_fusion = (f32[8,4,64]{2,1,0:T(4,128)S(1)}, f32[8,4,64,256]{3,2,1,0:T(8,128)}) fusion(pred[8,256]{1,0:T(8,128)(4,1)S(1)} %iota_compare_fusion, bf16[8,4,64,128]{3,2,1,0:T(8,128)(2,1)S(1)} %bitcast.38, bf16[8,256,4,128]{3,2,1,0:T(4,128)(2,1)S(1)} %copy-done), kind=kOutput, calls=%fused_computation.14 | convolution fusion | flops 135788544 | bytes 4728832 | tf_op jit(solution)/shard_map/rgmd,rkgd->rgmk/dot_general | solution.py:28
  32.5 17.6 %all-gather.3.cloned.1.call-done = bf16[16,64,4,128]{3,1,2,0:T(8,128)(2,1)} async-done(((bf16[1,64,4,128]{3,1,2,0:T(8,128)(2,1)}), bf16[16,64,4,128]{3,1,2,0:T(8,128)(2,1)}) %all-gather.3.cloned.1.call-update) | async-done | bytes 1048592 | tf_op jit(solution)/shard_map/all_gather | solution.py:44
  50.1 3.3 %gather_fusion = bf16[32,64,4,128]{3,1,2,0:T(8,128)(2,1)} fusion(bf16[16,64,4,128]{3,1,2,0:T(8,128)(2,1)} %all-gather.3.cloned.1.call-done, s32[1024]{0:T(1024)S(1)} %pad_clamp_fusion), kind=kCustom, calls=%fused_computation | custom fusion | bytes 4194432 | tf_op jit(solution)/shard_map/gather | solution.py:56
  53.5 1.8 %copy.72 = bf16[32,64,4,128]{3,1,0,2:T(8,128)(2,1)S(1)} copy(bf16[32,64,4,128]{3,1,2,0:T(8,128)(2,1)} %gather_fusion) | data formatting | bytes 4194304 | tf_op jit(solution)/shard_map/gather | solution.py:56
  55.2 0.0 copy-start.4
  55.2 2.2 %bitcast_reduce_fusion = (f32[8,4,64]{2,1,0:T(4,128)S(1)}, f32[8,4,256,64]{2,3,1,0:T(8,128)}) fusion(bf16[8,4,64,128]{3,2,1,0:T(8,128)(2,1)S(1)} %bitcast.39, bf16[8,256,4,128]{3,1,0,2:T(8,128)(2,1)S(1)} %bitcast.36), kind=kOutput, calls=%fused_computation.3 | convolution fusion | flops 135264256 | bytes 4726784 | tf_op jit(solution)/shard_map/rgmd,rkgd->rgmk/dot_general | solution.py:61
  57.4 0.1 fusion.33
  57.5 0.4 fusion.35
  57.8 31.3 %all-gather.5.cloned.1.call-done = bf16[16,64,4,128]{3,1,2,0:T(8,128)(2,1)} async-done(((bf16[1,64,4,128]{3,1,2,0:T(8,128)(2,1)}), bf16[16,64,4,128]{3,1,2,0:T(8,128)(2,1)}) %all-gather.5.cloned.1.call-update) | async-done | bytes 1048592 | tf_op jit(solution)/shard_map/all_gather | solution.py:45
  89.2 3.4 %gather_fusion.1 = bf16[32,64,4,128]{3,1,2,0:T(8,128)(2,1)} fusion(bf16[16,64,4,128]{3,1,2,0:T(8,128)(2,1)} %all-gather.5.cloned.1.call-done, s32[1024]{0:T(1024)S(1)} %pad_clamp_fusion), kind=kCustom, calls=%fused_computation.1 | custom fusion | bytes 4194432 | tf_op jit(solution)/shard_map/gather | solution.py:57
  92.5 1.9 %copy.77 = bf16[32,64,4,128]{3,1,0,2:T(8,128)(2,1)S(1)} copy(bf16[32,64,4,128]{3,1,2,0:T(8,128)(2,1)} %gather_fusion.1) | data formatting | bytes 4194304 | tf_op jit(solution)/shard_map/gather | solution.py:57
  94.5 0.3 copy-done.1
  94.7 0.6 copy-done.2
  95.4 1.6 %fusion.11 = (f32[8,4,64]{2,1,0:T(4,128)S(1)}, f32[8,4,64]{2,1,0:T(4,128)S(1)}) fusion(f32[8,4,64,256]{3,2,1,0:T(8,128)S(1)} %copy-done.1, f32[8,4,64]{2,1,0:T(4,128)S(1)} %bitcast.45, pred[8,256]{1,0:T(8,128)(4,1)S(1)} %iota_compare_fusion, f32[8,4,256,64]{2,3,1,0:T(8,128)S(1)} %copy-done.2), kind=kLoop, calls=%fused_computation.17 | loop fusion | flops 3665920 | bytes 4220928 | tf_op jit(solution)/shard_map/reduce_sum | solution.py:67
  97.0 0.0 copy-done.3
  97.0 0.9 fusion.13
  97.9 0.9 fusion.22
  98.8 0.9 copy.79
  (14 shorter events, 0.1 us)
Async XLA Ops:
  6.5 23.7 %copy-start = (bf16[8,256,4,128]{3,2,1,0:T(4,128)(2,1)S(1)}, bf16[8,256,4,128]{3,2,1,0:T(4,128)(2,1)}, u32[]{:S(2)}) copy-start(bf16[8,256,4,128]{3,2,1,0:T(4,128)(2,1)} %param.13) | copy-start | bytes 6291460
  6.5 43.6 %all-gather.3.cloned.1.call-start = ((), (), s32[]{:S(2)}) async-start(), calls=%async_computation | async-start | bytes 1114112 | tf_op jit(solution)/shard_map/all_gather | solution.py:44
  8.2 81.0 %all-gather.5.cloned.1.call-start = ((), (), s32[]{:S(2)}) async-start(), calls=%async_computation.1 | async-start | bytes 1114112 | tf_op jit(solution)/shard_map/all_gather | solution.py:45
  55.2 2.3 %copy-start.4 = (bf16[8,4,4,128]{3,2,1,0:T(4,128)(2,1)S(1)}, bf16[8,4,4,128]{3,2,1,0:T(4,128)(2,1)}, u32[]{:S(2)}) copy-start(bf16[8,4,4,128]{3,2,1,0:T(4,128)(2,1)} %param.12) | copy-start | bytes 98308
  92.5 2.2 %copy-start.1 = (f32[8,4,64,256]{3,2,1,0:T(8,128)S(1)}, f32[8,4,64,256]{3,2,1,0:T(8,128)}, u32[]{:S(2)}) copy-start(f32[8,4,64,256]{3,2,1,0:T(8,128)} %get-tuple-element.10) | copy-start | bytes 6291460
  92.5 2.9 %copy-start.2 = (f32[8,4,256,64]{2,3,1,0:T(8,128)S(1)}, f32[8,4,256,64]{2,3,1,0:T(8,128)}, u32[]{:S(2)}) copy-start(f32[8,4,256,64]{2,3,1,0:T(8,128)} %get-tuple-element.8) | copy-start | bytes 6291460
  95.4 1.6 %copy-start.3 = (bf16[8,256,4,128]{3,2,1,0:T(4,128)(2,1)S(1)}, bf16[8,256,4,128]{3,2,1,0:T(4,128)(2,1)}, u32[]{:S(2)}) copy-start(bf16[8,256,4,128]{3,2,1,0:T(4,128)(2,1)} %param.14) | copy-start | bytes 6291460
Sparse Core Ops, SparseCore 0:
  9.5 40.5 all-gather.2
  52.3 36.8 all-gather.4
where the time goes:
time: 107 us
  waiting for transfers between devices  49 us (46%)
  local copies, waits for them, and re-layouts  18.5 us (17%)
  between operations  14.2 us (13%)
  blocking collectives  13.8 us (13%)
  matrix products  7.74 us (7%)
  other arithmetic  3.32 us (3%)
    all_gather x1, waiting for transfers between devices, per_device(): lax.all_gather(prefix_values, 'loop', axis=0, tiled=True)  31.3 us
    all_gather x1, waiting for transfers between devices, per_device(): lax.all_gather(prefix_keys, 'loop', axis=0, tiled=True)  17.6 us
    unnamed x1, blocking collectives  13.8 us
    unnamed x15, local copies, waits for them, and re-layouts  6.01 us
    gather x2, local copies, waits for them, and re-layouts, per_device(): all_values[slots]  5.31 us
    gather x2, local copies, waits for them, and re-layouts, per_device(): all_keys[slots]  5.09 us
    dot_general x1, matrix products, per_device(): jnp.einsum('rgmd,rkgd->rgmk', grouped, suffix_keys, preferred_element_typ...  2.22 us
    dot_general x1, matrix products, per_device(): jnp.einsum('rgmd,rkgd->rgmk', grouped, prior_keys, preferred_element_type...  2.16 us
  transfers between devices with their start and end apart: 2, of which 2 were waited for; matrix products, arithmetic and copies ran while one was open for 16% of the time, Pallas kernels for 0%

commit v1 on v0

--- a/solution.py
+++ b/solution.py
@@ -3,6 +3,24 @@
 import jax.numpy as jnp
 from jax import lax
 from jax.sharding import PartitionSpec as P
+
+
+def gather_around(value, axis, dim):
+    ways, here, step = (lax.axis_size(axis), lax.axis_index(axis), value.shape[dim])
+    shape = [n * ways if d == dim else n for d, n in enumerate(value.shape)]
+    full = lax.dynamic_update_slice_in_dim(
+        jnp.zeros(shape, value.dtype), value, here * step, axis=dim
+    )
+    going_up = going_down = value
+    for far in range(1, ways // 2 + 1):
+        going_up = lax.ppermute(going_up, axis, [(d, (d + 1) % ways) for d in range(ways)])
+        full = lax.dynamic_update_slice_in_dim(full, going_up, (here - far) % ways * step, axis=dim)
+        if 2 * far < ways:
+            going_down = lax.ppermute(going_down, axis, [(d, (d - 1) % ways) for d in range(ways)])
+            full = lax.dynamic_update_slice_in_dim(
+                full, going_down, (here + far) % ways * step, axis=dim
+            )
+    return full
 
 
 def per_device(
@@ -42,7 +60,7 @@
     )
     gathered = (
         lax.all_gather(prefix_keys, "loop", axis=0, tiled=True),
-        lax.all_gather(prefix_values, "loop", axis=0, tiled=True),
+        gather_around(prefix_values, "loop", 0),
         lax.all_gather(block_ids, "loop", axis=0, tiled=True),
     )
     all_keys, all_values, all_ids = gathered

time: 107 us -> 105 us (0.981)
  starting transfers between devices: 0.04 us -> 32.6 us
  waiting for transfers between devices: 49 us -> 18.2 us
  blocking collectives: 13.8 us -> 10.2 us
    ppermute x0 -> x15, starting transfers between devices: none -> 32.6 us  [the longest x7 32 us: gather_around(): lax.ppermute(going_down, axis, [(d, (d - 1) % ways) for d in range(ways)])]
    all_gather x1 -> x0, waiting for transfers between devices: 31.3 us -> none  [per_device(): lax.all_gather(prefix_values, 'loop', axis=0, tiled=True)]
    ppermute x0 -> x15, waiting for transfers between devices: none -> 18.2 us  [the longest x8 18.1 us: gather_around(): lax.ppermute(going_up, axis, [(d, (d + 1) % ways) for d in range(ways)])]
    all_gather x1, waiting for transfers between devices: 17.6 us -> 0.01 us  [per_device(): lax.all_gather(prefix_keys, 'loop', axis=0, tiled=True)]
    unnamed x1, blocking collectives: 13.8 us -> 10.2 us
    dot_general x1, matrix products: 2.16 us -> 0.95 us  [per_device(): jnp.einsum('rgmd,rkgd->rgmk', grouped, prior_keys, preferred_element_type...]
    dot_general x1, matrix products: 2.22 us -> 3.32 us  [per_device(): jnp.einsum('rgmd,rkgd->rgmk', grouped, suffix_keys, preferred_element_typ...]
    unnamed x15 -> x21, local copies, waits for them, and re-layouts: 6.01 us -> 5.32 us
  transfers between devices with their start and end apart: 2 -> 16, of which waited for: 2 -> 8; matrix products, arithmetic and copies ran while one was open for 16% -> 16% of each run, Pallas kernels for 0% -> 0%
where the time goes in v1:
time: 105 us
  starting transfers between devices  32.6 us (31%)
  local copies, waits for them, and re-layouts  19.2 us (18%)
  waiting for transfers between devices  18.2 us (17%)
  between operations  14.5 us (14%)
  blocking collectives  10.2 us (10%)
  matrix products  6.85 us (7%)
  other arithmetic  3.31 us (3%)
    ppermute x7, starting transfers between devices, gather_around(): lax.ppermute(going_down, axis, [(d, (d - 1) % ways) for d in range(ways)])  32 us
    ppermute x8, waiting for transfers between devices, gather_around(): lax.ppermute(going_up, axis, [(d, (d + 1) % ways) for d in range(ways)])  18.1 us
    unnamed x1, blocking collectives  10.2 us
    unnamed x21, local copies, waits for them, and re-layouts  5.32 us
    gather x2, local copies, waits for them, and re-layouts, per_device(): all_values[slots]  5.27 us
    gather x2, local copies, waits for them, and re-layouts, per_device(): all_keys[slots]  5.21 us
    dot_general x1, matrix products, per_device(): jnp.einsum('rgmd,rkgd->rgmk', grouped, suffix_keys, preferred_element_typ...  3.32 us
  transfers between devices with their start and end apart: 16, of which 8 were waited for; matrix products, arithmetic and copies ran while one was open for 16% of the time, Pallas kernels for 0%

profile of v1, /device:TPU:0, one launch (start us, length us, event | category | flops | bytes accessed | tf_op | source)
XLA Modules:
  0.0 104.9 jit_solution(13549708355018907389)
XLA Ops:
  6.8 1.0 fusion.46
  8.3 5.0 %collective-permute-start.1 = (bf16[1,64,4,128]{3,1,2,0:T(8,128)(2,1)S(1)}, bf16[1,64,4,128]{3,1,2,0:T(8,128)(2,1)S(1)}, u32[]{:S(2)}, u32[]{:S(2)}) collective-permute-start(bf16[1,64,4,128]{3,1,2,0:T(8,128)(2,1)S(1)} %get-tuple-element.7), channel_id=1, source_target_pairs={{0,15},{1,0},{2,1},{3,2},{4,3},{5,4},{6,5},{7,6},{8,7},{9,8},{10,9... | collective-permute-start | bytes 196616 | tf_op jit(solution)/shard_map/ppermute | solution.py:19
  13.4 1.5 %copy.92 = bf16[1,64,4,128]{3,1,2,0:T(8,128)(2,1)} copy(bf16[1,64,4,128]{3,2,1,0:T(4,128)(2,1)} %param.16) | data formatting | bytes 131072 | tf_op args[6]
  15.8 1.2 %dynamic-slice = u32[1]{0:T(128)} dynamic-slice(u32[32]{0:T(128)} %constant.140, u32[]{:T(128)S(6)} %add.202), dynamic_slice_sizes={1} | dynamic-slice | bytes 12
  17.0 0.8 dynamic-update-slice
  17.8 10.2 %all-reduce = s32[16]{0:T(128)S(1)} all-reduce(s32[16]{0:T(128)S(1)} %dynamic-update-slice), channel_id=1, replica_groups=mesh['groups'=2,'loop'=16] {'loop'}, use_global_device_ids=true, to_apply=%add | all-reduce | flops 16 | bytes 128
  28.0 0.9 select_reduce_fusion.2
  28.9 0.7 iota_compare_fusion
  29.8 1.9 %copy.89 = bf16[8,4,4,16,128]{4,3,2,1,0:T(8,128)(2,1)} copy(bf16[8,4,4,16,128]{4,3,1,2,0:T(8,128)(2,1)} %bitcast.41) | data formatting | bytes 1048576 | tf_op jit(solution)/shard_map/transpose | solution.py:44
  31.7 3.3 %select_reduce_fusion = (f32[8,4,64]{2,1,0:T(4,128)S(1)}, f32[8,4,64,256]{3,2,1,0:T(8,128)}) fusion(pred[8,256]{1,0:T(8,128)(4,1)S(1)} %iota_compare_fusion, bf16[8,4,64,128]{3,2,1,0:T(8,128)(2,1)} %bitcast.37, bf16[8,256,4,128]{3,2,1,0:T(4,128)(2,1)S(1)} %copy-done), kind=kOutput, calls=%fused_computation.14 | convolution fusion | flops 135788544 | bytes 4728832 | tf_op jit(solution)/shard_map/rgmd,rkgd->rgmk/dot_general | solution.py:46
  35.5 4.4 %collective-permute-start.3 = (bf16[1,64,4,128]{3,1,2,0:T(8,128)(2,1)S(1)}, bf16[1,64,4,128]{3,1,2,0:T(8,128)(2,1)S(1)}, u32[]{:S(2)}, u32[]{:S(2)}) collective-permute-start(bf16[1,64,4,128]{3,1,2,0:T(8,128)(2,1)S(1)} %collective-permute-done.1), channel_id=1, source_target_pairs={{0,15},{1,0},{2,1},{3,2},{4,3},{5,4},{6,5},{7,6},{8,7},{9,8},{10,9... | collective-permute-start | bytes 196616 | tf_op jit(solution)/shard_map/ppermute | solution.py:19
  40.0 2.0 %collective-permute-done.2 = bf16[1,64,4,128]{3,1,2,0:T(8,128)(2,1)S(1)} collective-permute-done((bf16[1,64,4,128]{3,1,2,0:T(8,128)(2,1)S(1)}, bf16[1,64,4,128]{3,1,2,0:T(8,128)(2,1)S(1)}, u32[]{:S(2)}, u32[]{:S(2)}) %collective-permute-start.2) | collective-permute-done | bytes 65568 | tf_op jit(solution)/shard_map/ppermute | solution.py:16
  42.1 4.6 %collective-permute-start.5 = (bf16[1,64,4,128]{3,1,2,0:T(8,128)(2,1)S(1)}, bf16[1,64,4,128]{3,1,2,0:T(8,128)(2,1)S(1)}, u32[]{:S(2)}, u32[]{:S(2)}) collective-permute-start(bf16[1,64,4,128]{3,1,2,0:T(8,128)(2,1)S(1)} %collective-permute-done.3), channel_id=1, source_target_pairs={{0,15},{1,0},{2,1},{3,2},{4,3},{5,4},{6,5},{7,6},{8,7},{9,8},{10,9... | collective-permute-start | bytes 196616 | tf_op jit(solution)/shard_map/ppermute | solution.py:19
  46.7 2.3 %collective-permute-done.4 = bf16[1,64,4,128]{3,1,2,0:T(8,128)(2,1)S(1)} collective-permute-done((bf16[1,64,4,128]{3,1,2,0:T(8,128)(2,1)S(1)}, bf16[1,64,4,128]{3,1,2,0:T(8,128)(2,1)S(1)}, u32[]{:S(2)}, u32[]{:S(2)}) %collective-permute-start.4) | collective-permute-done | bytes 65568 | tf_op jit(solution)/shard_map/ppermute | solution.py:16
  49.0 4.4 %collective-permute-start.7 = (bf16[1,64,4,128]{3,1,2,0:T(8,128)(2,1)S(1)}, bf16[1,64,4,128]{3,1,2,0:T(8,128)(2,1)S(1)}, u32[]{:S(2)}, u32[]{:S(2)}) collective-permute-start(bf16[1,64,4,128]{3,1,2,0:T(8,128)(2,1)S(1)} %collective-permute-done.5), channel_id=1, source_target_pairs={{0,15},{1,0},{2,1},{3,2},{4,3},{5,4},{6,5},{7,6},{8,7},{9,8},{10,9... | collective-permute-start | bytes 196616 | tf_op jit(solution)/shard_map/ppermute | solution.py:19
  53.5 1.9 %collective-permute-done.6 = bf16[1,64,4,128]{3,1,2,0:T(8,128)(2,1)S(1)} collective-permute-done((bf16[1,64,4,128]{3,1,2,0:T(8,128)(2,1)S(1)}, bf16[1,64,4,128]{3,1,2,0:T(8,128)(2,1)S(1)}, u32[]{:S(2)}, u32[]{:S(2)}) %collective-permute-start.6) | collective-permute-done | bytes 65568 | tf_op jit(solution)/shard_map/ppermute | solution.py:16
  55.4 4.5 %collective-permute-start.9 = (bf16[1,64,4,128]{3,1,2,0:T(8,128)(2,1)S(1)}, bf16[1,64,4,128]{3,1,2,0:T(8,128)(2,1)S(1)}, u32[]{:S(2)}, u32[]{:S(2)}) collective-permute-start(bf16[1,64,4,128]{3,1,2,0:T(8,128)(2,1)S(1)} %collective-permute-done.7), channel_id=1, source_target_pairs={{0,15},{1,0},{2,1},{3,2},{4,3},{5,4},{6,5},{7,6},{8,7},{9,8},{10,9... | collective-permute-start | bytes 196616 | tf_op jit(solution)/shard_map/ppermute | solution.py:19
  59.9 1.8 %collective-permute-done.8 = bf16[1,64,4,128]{3,1,2,0:T(8,128)(2,1)S(1)} collective-permute-done((bf16[1,64,4,128]{3,1,2,0:T(8,128)(2,1)S(1)}, bf16[1,64,4,128]{3,1,2,0:T(8,128)(2,1)S(1)}, u32[]{:S(2)}, u32[]{:S(2)}) %collective-permute-start.8) | collective-permute-done | bytes 65568 | tf_op jit(solution)/shard_map/ppermute | solution.py:16
  61.8 4.5 %collective-permute-start.11 = (bf16[1,64,4,128]{3,1,2,0:T(8,128)(2,1)S(1)}, bf16[1,64,4,128]{3,1,2,0:T(8,128)(2,1)S(1)}, u32[]{:S(2)}, u32[]{:S(2)}) collective-permute-start(bf16[1,64,4,128]{3,1,2,0:T(8,128)(2,1)S(1)} %collective-permute-done.9), channel_id=1, source_target_pairs={{0,15},{1,0},{2,1},{3,2},{4,3},{5,4},{6,5},{7,6},{8,7},{9,8},{10,9... | collective-permute-start | bytes 196616 | tf_op jit(solution)/shard_map/ppermute | solution.py:19
  66.3 1.8 %collective-permute-done.10 = bf16[1,64,4,128]{3,1,2,0:T(8,128)(2,1)S(1)} collective-permute-done((bf16[1,64,4,128]{3,1,2,0:T(8,128)(2,1)S(1)}, bf16[1,64,4,128]{3,1,2,0:T(8,128)(2,1)S(1)}, u32[]{:S(2)}, u32[]{:S(2)}) %collective-permute-start.10) | collective-permute-done | bytes 65568 | tf_op jit(solution)/shard_map/ppermute | solution.py:16
  68.2 4.5 %collective-permute-start.13 = (bf16[1,64,4,128]{3,1,2,0:T(8,128)(2,1)S(1)}, bf16[1,64,4,128]{3,1,2,0:T(8,128)(2,1)S(1)}, u32[]{:S(2)}, u32[]{:S(2)}) collective-permute-start(bf16[1,64,4,128]{3,1,2,0:T(8,128)(2,1)S(1)} %collective-permute-done.11), channel_id=1, source_target_pairs={{0,15},{1,0},{2,1},{3,2},{4,3},{5,4},{6,5},{7,6},{8,7},{9,8},{10,9... | collective-permute-start | bytes 196616 | tf_op jit(solution)/shard_map/ppermute | solution.py:19
  72.7 1.8 %collective-permute-done.12 = bf16[1,64,4,128]{3,1,2,0:T(8,128)(2,1)S(1)} collective-permute-done((bf16[1,64,4,128]{3,1,2,0:T(8,128)(2,1)S(1)}, bf16[1,64,4,128]{3,1,2,0:T(8,128)(2,1)S(1)}, u32[]{:S(2)}, u32[]{:S(2)}) %collective-permute-start.12) | collective-permute-done | bytes 65568 | tf_op jit(solution)/shard_map/ppermute | solution.py:16
  74.6 6.3 %collective-permute-done.14 = bf16[1,64,4,128]{3,1,2,0:T(8,128)(2,1)S(1)} collective-permute-done((bf16[1,64,4,128]{3,1,2,0:T(8,128)(2,1)S(1)}, bf16[1,64,4,128]{3,1,2,0:T(8,128)(2,1)S(1)}, u32[]{:S(2)}, u32[]{:S(2)}) %collective-permute-start.14) | collective-permute-done | bytes 65568 | tf_op jit(solution)/shard_map/ppermute | solution.py:16
  81.0 2.1 %gather_fusion.1 = bf16[32,64,4,128]{3,1,2,0:T(8,128)(2,1)} fusion(bf16[16,64,4,128]{3,1,2,0:T(8,128)(2,1)S(1)} %constant_dynamic-update-slice_fusion, s32[1024]{0:T(1024)S(1)} %pad_clamp_fusion), kind=kCustom, calls=%fused_computation.1 | custom fusion | bytes 4194432 | tf_op jit(solution)/shard_map/gather | solution.py:75
  83.1 3.1 %copy.101 = bf16[32,64,4,128]{3,1,0,2:T(8,128)(2,1)} copy(bf16[32,64,4,128]{3,1,2,0:T(8,128)(2,1)} %gather_fusion.1) | data formatting | bytes 4194304 | tf_op jit(solution)/shard_map/gather | solution.py:75
  86.2 3.4 %gather_fusion = bf16[32,64,4,128]{3,1,2,0:T(8,128)(2,1)} fusion(bf16[16,64,4,128]{3,1,2,0:T(8,128)(2,1)} %all-gather.2.cloned.1.call-done, s32[1024]{0:T(1024)S(1)} %pad_clamp_fusion), kind=kCustom, calls=%fused_computation | custom fusion | bytes 4194432 | tf_op jit(solution)/shard_map/gather | solution.py:74
  89.6 1.8 %copy.94 = bf16[32,64,4,128]{3,1,0,2:T(8,128)(2,1)S(1)} copy(bf16[32,64,4,128]{3,1,2,0:T(8,128)(2,1)} %gather_fusion) | data formatting | bytes 4194304 | tf_op jit(solution)/shard_map/gather | solution.py:74
  91.5 0.9 bitcast_reduce_fusion
  93.1 1.6 %fusion.11 = (f32[8,4,64]{2,1,0:T(4,128)S(1)}, f32[8,4,64]{2,1,0:T(4,128)S(1)}) fusion(f32[8,4,64,256]{3,2,1,0:T(8,128)S(1)} %copy-done.1, f32[8,4,64]{2,1,0:T(4,128)S(1)} %bitcast.45, pred[8,256]{1,0:T(8,128)(4,1)S(1)} %iota_compare_fusion, f32[8,4,256,64]{2,3,1,0:T(8,128)S(1)} %get-tuple-element.10), kind=kLoop, calls=%fused_computation.17 | loop fusion | flops 3665920 | bytes 4220928 | tf_op jit(solution)/shard_map/reduce_sum | solution.py:85
  94.7 0.9 fusion.13
  96.3 0.9 fusion.22
  97.2 0.9 copy.103
  (63 shorter events, 3.2 us)
Async XLA Ops:
  6.5 25.2 %copy-start = (bf16[8,256,4,128]{3,2,1,0:T(4,128)(2,1)S(1)}, bf16[8,256,4,128]{3,2,1,0:T(4,128)(2,1)}, u32[]{:S(2)}) copy-start(bf16[8,256,4,128]{3,2,1,0:T(4,128)(2,1)} %param.13) | copy-start | bytes 6291460
  6.5 79.7 %all-gather.2.cloned.1.call-start = ((), (), s32[]{:S(2)}) async-start(), calls=%async_computation | async-start | bytes 1114112 | tf_op jit(solution)/shard_map/all_gather | solution.py:62
  7.8 27.7 %collective-permute-start = (bf16[1,64,4,128]{3,1,2,0:T(8,128)(2,1)S(1)}, bf16[1,64,4,128]{3,1,2,0:T(8,128)(2,1)S(1)}, u32[]{:S(2)}, u32[]{:S(2)}) collective-permute-start(bf16[1,64,4,128]{3,1,2,0:T(8,128)(2,1)S(1)} %get-tuple-element.7), channel_id=1, source_target_pairs={{0,1},{1,2},{2,3},{3,4},{4,5},{5,6},{6,7},{7,8},{8,9},{9,10},{10,1... | collective-permute-start | bytes 196616 | tf_op jit(solution)/shard_map/ppermute | solution.py:16
  8.3 27.2 %collective-permute-start.1 = (bf16[1,64,4,128]{3,1,2,0:T(8,128)(2,1)S(1)}, bf16[1,64,4,128]{3,1,2,0:T(8,128)(2,1)S(1)}, u32[]{:S(2)}, u32[]{:S(2)}) collective-permute-start(bf16[1,64,4,128]{3,1,2,0:T(8,128)(2,1)S(1)} %get-tuple-element.7), channel_id=1, source_target_pairs={{0,15},{1,0},{2,1},{3,2},{4,3},{5,4},{6,5},{7,6},{8,7},{9,8},{10,9... | collective-permute-start | bytes 196616 | tf_op jit(solution)/shard_map/ppermute | solution.py:19
  31.7 3.3 %copy-start.2 = (bf16[8,4,4,16,128]{4,3,2,1,0:T(8,128)(2,1)S(1)}, bf16[8,4,4,16,128]{4,3,2,1,0:T(8,128)(2,1)}, u32[]{:S(2)}) copy-start(bf16[8,4,4,16,128]{4,3,2,1,0:T(8,128)(2,1)} %copy.89) | copy-start | bytes 1572868
  31.7 3.3 %copy-start.7 = (bf16[8,4,4,128]{3,2,1,0:T(4,128)(2,1)S(1)}, bf16[8,4,4,128]{3,2,1,0:T(4,128)(2,1)}, u32[]{:S(2)}) copy-start(bf16[8,4,4,128]{3,2,1,0:T(4,128)(2,1)} %param.11) | copy-start | bytes 98308
  35.5 6.6 %collective-permute-start.2 = (bf16[1,64,4,128]{3,1,2,0:T(8,128)(2,1)S(1)}, bf16[1,64,4,128]{3,1,2,0:T(8,128)(2,1)S(1)}, u32[]{:S(2)}, u32[]{:S(2)}) collective-permute-start(bf16[1,64,4,128]{3,1,2,0:T(8,128)(2,1)S(1)} %collective-permute-done), channel_id=1, source_target_pairs={{0,1},{1,2},{2,3},{3,4},{4,5},{5,6},{6,7},{7,8},{8,9},{9,10},{10,1... | collective-permute-start | bytes 196616 | tf_op jit(solution)/shard_map/ppermute | solution.py:16
  35.5 6.6 %collective-permute-start.3 = (bf16[1,64,4,128]{3,1,2,0:T(8,128)(2,1)S(1)}, bf16[1,64,4,128]{3,1,2,0:T(8,128)(2,1)S(1)}, u32[]{:S(2)}, u32[]{:S(2)}) collective-permute-start(bf16[1,64,4,128]{3,1,2,0:T(8,128)(2,1)S(1)} %collective-permute-done.1), channel_id=1, source_target_pairs={{0,15},{1,0},{2,1},{3,2},{4,3},{5,4},{6,5},{7,6},{8,7},{9,8},{10,9... | collective-permute-start | bytes 196616 | tf_op jit(solution)/shard_map/ppermute | solution.py:19
  42.0 7.0 %collective-permute-start.4 = (bf16[1,64,4,128]{3,1,2,0:T(8,128)(2,1)S(1)}, bf16[1,64,4,128]{3,1,2,0:T(8,128)(2,1)S(1)}, u32[]{:S(2)}, u32[]{:S(2)}) collective-permute-start(bf16[1,64,4,128]{3,1,2,0:T(8,128)(2,1)S(1)} %collective-permute-done.2), channel_id=1, source_target_pairs={{0,1},{1,2},{2,3},{3,4},{4,5},{5,6},{6,7},{7,8},{8,9},{9,10},{10,1... | collective-permute-start | bytes 196616 | tf_op jit(solution)/shard_map/ppermute | solution.py:16
  42.1 6.9 %collective-permute-start.5 = (bf16[1,64,4,128]{3,1,2,0:T(8,128)(2,1)S(1)}, bf16[1,64,4,128]{3,1,2,0:T(8,128)(2,1)S(1)}, u32[]{:S(2)}, u32[]{:S(2)}) collective-permute-start(bf16[1,64,4,128]{3,1,2,0:T(8,128)(2,1)S(1)} %collective-permute-done.3), channel_id=1, source_target_pairs={{0,15},{1,0},{2,1},{3,2},{4,3},{5,4},{6,5},{7,6},{8,7},{9,8},{10,9... | collective-permute-start | bytes 196616 | tf_op jit(solution)/shard_map/ppermute | solution.py:19
  49.0 6.4 %collective-permute-start.6 = (bf16[1,64,4,128]{3,1,2,0:T(8,128)(2,1)S(1)}, bf16[1,64,4,128]{3,1,2,0:T(8,128)(2,1)S(1)}, u32[]{:S(2)}, u32[]{:S(2)}) collective-permute-start(bf16[1,64,4,128]{3,1,2,0:T(8,128)(2,1)S(1)} %collective-permute-done.4), channel_id=1, source_target_pairs={{0,1},{1,2},{2,3},{3,4},{4,5},{5,6},{6,7},{7,8},{8,9},{9,10},{10,1... | collective-permute-start | bytes 196616 | tf_op jit(solution)/shard_map/ppermute | solution.py:16
  49.0 6.4 %collective-permute-start.7 = (bf16[1,64,4,128]{3,1,2,0:T(8,128)(2,1)S(1)}, bf16[1,64,4,128]{3,1,2,0:T(8,128)(2,1)S(1)}, u32[]{:S(2)}, u32[]{:S(2)}) collective-permute-start(bf16[1,64,4,128]{3,1,2,0:T(8,128)(2,1)S(1)} %collective-permute-done.5), channel_id=1, source_target_pairs={{0,15},{1,0},{2,1},{3,2},{4,3},{5,4},{6,5},{7,6},{8,7},{9,8},{10,9... | collective-permute-start | bytes 196616 | tf_op jit(solution)/shard_map/ppermute | solution.py:19
  55.4 6.4 %collective-permute-start.8 = (bf16[1,64,4,128]{3,1,2,0:T(8,128)(2,1)S(1)}, bf16[1,64,4,128]{3,1,2,0:T(8,128)(2,1)S(1)}, u32[]{:S(2)}, u32[]{:S(2)}) collective-permute-start(bf16[1,64,4,128]{3,1,2,0:T(8,128)(2,1)S(1)} %collective-permute-done.6), channel_id=1, source_target_pairs={{0,1},{1,2},{2,3},{3,4},{4,5},{5,6},{6,7},{7,8},{8,9},{9,10},{10,1... | collective-permute-start | bytes 196616 | tf_op jit(solution)/shard_map/ppermute | solution.py:16
  55.4 6.4 %collective-permute-start.9 = (bf16[1,64,4,128]{3,1,2,0:T(8,128)(2,1)S(1)}, bf16[1,64,4,128]{3,1,2,0:T(8,128)(2,1)S(1)}, u32[]{:S(2)}, u32[]{:S(2)}) collective-permute-start(bf16[1,64,4,128]{3,1,2,0:T(8,128)(2,1)S(1)} %collective-permute-done.7), channel_id=1, source_target_pairs={{0,15},{1,0},{2,1},{3,2},{4,3},{5,4},{6,5},{7,6},{8,7},{9,8},{10,9... | collective-permute-start | bytes 196616 | tf_op jit(solution)/shard_map/ppermute | solution.py:19
  61.8 6.4 %collective-permute-start.10 = (bf16[1,64,4,128]{3,1,2,0:T(8,128)(2,1)S(1)}, bf16[1,64,4,128]{3,1,2,0:T(8,128)(2,1)S(1)}, u32[]{:S(2)}, u32[]{:S(2)}) collective-permute-start(bf16[1,64,4,128]{3,1,2,0:T(8,128)(2,1)S(1)} %collective-permute-done.8), channel_id=1, source_target_pairs={{0,1},{1,2},{2,3},{3,4},{4,5},{5,6},{6,7},{7,8},{8,9},{9,10},{10,1... | collective-permute-start | bytes 196616 | tf_op jit(solution)/shard_map/ppermute | solution.py:16
  61.8 6.4 %collective-permute-start.11 = (bf16[1,64,4,128]{3,1,2,0:T(8,128)(2,1)S(1)}, bf16[1,64,4,128]{3,1,2,0:T(8,128)(2,1)S(1)}, u32[]{:S(2)}, u32[]{:S(2)}) collective-permute-start(bf16[1,64,4,128]{3,1,2,0:T(8,128)(2,1)S(1)} %collective-permute-done.9), channel_id=1, source_target_pairs={{0,15},{1,0},{2,1},{3,2},{4,3},{5,4},{6,5},{7,6},{8,7},{9,8},{10,9... | collective-permute-start | bytes 196616 | tf_op jit(solution)/shard_map/ppermute | solution.py:19
  68.2 6.4 %collective-permute-start.12 = (bf16[1,64,4,128]{3,1,2,0:T(8,128)(2,1)S(1)}, bf16[1,64,4,128]{3,1,2,0:T(8,128)(2,1)S(1)}, u32[]{:S(2)}, u32[]{:S(2)}) collective-permute-start(bf16[1,64,4,128]{3,1,2,0:T(8,128)(2,1)S(1)} %collective-permute-done.10), channel_id=1, source_target_pairs={{0,1},{1,2},{2,3},{3,4},{4,5},{5,6},{6,7},{7,8},{8,9},{9,10},{10,1... | collective-permute-start | bytes 196616 | tf_op jit(solution)/shard_map/ppermute | solution.py:16
  68.2 6.4 %collective-permute-start.13 = (bf16[1,64,4,128]{3,1,2,0:T(8,128)(2,1)S(1)}, bf16[1,64,4,128]{3,1,2,0:T(8,128)(2,1)S(1)}, u32[]{:S(2)}, u32[]{:S(2)}) collective-permute-start(bf16[1,64,4,128]{3,1,2,0:T(8,128)(2,1)S(1)} %collective-permute-done.11), channel_id=1, source_target_pairs={{0,15},{1,0},{2,1},{3,2},{4,3},{5,4},{6,5},{7,6},{8,7},{9,8},{10,9... | collective-permute-start | bytes 196616 | tf_op jit(solution)/shard_map/ppermute | solution.py:19
  74.6 6.4 %collective-permute-start.14 = (bf16[1,64,4,128]{3,1,2,0:T(8,128)(2,1)S(1)}, bf16[1,64,4,128]{3,1,2,0:T(8,128)(2,1)S(1)}, u32[]{:S(2)}, u32[]{:S(2)}) collective-permute-start(bf16[1,64,4,128]{3,1,2,0:T(8,128)(2,1)S(1)} %collective-permute-done.12), channel_id=1, source_target_pairs={{0,1},{1,2},{2,3},{3,4},{4,5},{5,6},{6,7},{7,8},{8,9},{9,10},{10,1... | collective-permute-start | bytes 196616 | tf_op jit(solution)/shard_map/ppermute | solution.py:16
  89.6 1.9 %copy-start.3 = (bf16[8,4,4,16,128]{4,3,2,1,0:T(8,128)(2,1)S(1)}, bf16[8,4,4,16,128]{4,3,2,1,0:T(8,128)(2,1)}, u32[]{:S(2)}) copy-start(bf16[8,4,4,16,128]{4,3,2,1,0:T(8,128)(2,1)} %copy.89) | copy-start | bytes 1572868
  91.5 1.1 %copy-start.6 = (bf16[8,4,4,128]{3,2,1,0:T(4,128)(2,1)S(1)}, bf16[8,4,4,128]{3,2,1,0:T(4,128)(2,1)}, u32[]{:S(2)}) copy-start(bf16[8,4,4,128]{3,2,1,0:T(4,128)(2,1)} %param.12) | copy-start | bytes 98308
  91.5 1.6 %copy-start.1 = (f32[8,4,64,256]{3,2,1,0:T(8,128)S(1)}, f32[8,4,64,256]{3,2,1,0:T(8,128)}, u32[]{:S(2)}) copy-start(f32[8,4,64,256]{3,2,1,0:T(8,128)} %get-tuple-element.12) | copy-start | bytes 6291460
  93.1 1.6 %copy-start.4 = (bf16[8,256,4,128]{3,2,1,0:T(4,128)(2,1)S(1)}, bf16[8,256,4,128]{3,2,1,0:T(4,128)(2,1)}, u32[]{:S(2)}) copy-start(bf16[8,256,4,128]{3,2,1,0:T(4,128)(2,1)} %param.14) | copy-start | bytes 6291460
  94.7 1.6 %copy-start.5 = (bf16[32,64,4,128]{3,1,0,2:T(8,128)(2,1)S(1)}, bf16[32,64,4,128]{3,1,0,2:T(8,128)(2,1)}, u32[]{:S(2)}) copy-start(bf16[32,64,4,128]{3,1,0,2:T(8,128)(2,1)} %copy.101) | copy-start | bytes 6291460
Sparse Core Ops, SparseCore 0:
  15.0 36.9 all-gather.1
